TPU v7x, 32 devices: a whole 2x2x4 slice. The times are simulated.
32 devices in a mesh: expert: 8 (over y, x, core), replica: 4 (over z).
Axes of the slice: x: 2, y: 2, z: 4, core: 2. Of those that a mesh axis runs over, the one named last changes fastest.
Arguments:
- tokens: bfloat16 [8192, 7168], P(('expert', 'replica')), may hold values from -40 to 40
- routes: int32 [8192, 8], P(('expert', 'replica')), may hold values from 0 to 255, all different within a row
- gate_weight: bfloat16 [7168, 4096], P(None, 'expert'), may hold values from -0.0625 to 0.0625
- up_weight: bfloat16 [7168, 4096], P(None, 'expert'), may hold values from -0.0625 to 0.0625
Outputs:
- calibrated: bfloat16 [512, 4096], P(('expert', 'replica'))
Inputs may be any that keep to these rules, and one draw needn't show every extreme that they name: `routes`: each row names 8 different experts of the layer, and every expert is named by some row.
All inputs are finite; a program needn't handle non-finite values.
Results may differ from a plain program's by a relative error of at most 0.001.
Values may be sent and summed in bfloat16 or wider, within the bound.
A program may use at most 128 MiB of HBM per device.

v0:
```python
import math
import jax
import jax.numpy as jnp
from jax import lax
from jax.sharding import PartitionSpec as P

D = 7168
HSPLIT = 4
CAP = 16
KMOM = 12
QITERS = 4
QUANTILE_LEVEL = 0.99
EPSILON = 1e-06


def build_slots(routes, experts):
    window = jnp.arange(experts, dtype=jnp.int32)
    naming = jnp.sum((routes[:, :, None] == window[None, None, :]).astype(jnp.int32), axis=1)
    before = jnp.cumsum(naming, axis=0) - naming
    positions = jnp.arange(CAP, dtype=jnp.int32)
    chosen = naming[:, :, None] * (before[:, :, None] == positions[None, None, :]).astype(jnp.int32)
    token_ids = jnp.arange(routes.shape[0], dtype=jnp.int32)
    picked = jnp.sum(chosen * token_ids[:, None, None], axis=0)
    filled = jnp.sum(chosen, axis=0)
    return (picked, filled)


def chebyshev_sums(scaled, occupied):
    previous = jnp.ones_like(scaled)
    current = scaled
    totals = [
        jnp.sum(occupied[:, None] * previous, axis=0),
        jnp.sum(occupied[:, None] * current, axis=0),
    ]
    for degree in range(2, KMOM):
        previous, current = (current, 2.0 * scaled * current - previous)
        totals.append(jnp.sum(occupied[:, None] * current, axis=0))
    return jnp.stack(totals[:KMOM])


def clip_fraction(moments, counted):
    coefficient = moments[1:] / counted[None, :]
    orders = jnp.arange(1, KMOM, dtype=jnp.float32)[:, None]
    angles = jnp.full(moments.shape[1:], 0.5 * math.pi, jnp.float32)
    for iteration in range(QITERS):
        lower_mass = (
            1.0
            - angles / math.pi
            - 2.0
            / math.pi
            * jnp.sum(coefficient * jnp.sin(orders * angles[None, :]) / orders, axis=0)
        )
        angles = angles + math.pi * (lower_mass - QUANTILE_LEVEL)
    return 0.5 * (1.0 + jnp.cos(angles))


def shards(tokens, routes, gate_weight, up_weight):
    devices_e = lax.axis_size("expert")
    experts = devices_e // HSPLIT
    shard_width = gate_weight.shape[1]
    picked, filled = build_slots(routes, experts)
    occupied = filled.astype(jnp.bfloat16)
    gathered = jnp.take(tokens, picked.reshape(-1), axis=0).reshape(experts, CAP, D)
    gathered = gathered * occupied[:, :, None]
    outgoing = jnp.repeat(gathered, HSPLIT, axis=0)
    presence = jnp.repeat(occupied, HSPLIT, axis=0)
    received = lax.all_to_all(outgoing, "expert", split_axis=0, concat_axis=0, tiled=True)
    flat_rows = received.reshape(-1, D)
    gate_act = jnp.dot(flat_rows, gate_weight, preferred_element_type=jnp.float32)
    up_act = jnp.dot(flat_rows, up_weight, preferred_element_type=jnp.float32)
    hidden = jax.nn.silu(gate_act) * up_act
    hidden, present = (
        hidden.reshape(received.shape[:-1] + (shard_width,)),
        lax.all_to_all(presence, "expert", split_axis=0, concat_axis=0, tiled=True),
    )
    magnitude = jnp.abs(hidden)
    ceiling = lax.pmax(jnp.max(magnitude, axis=(0, 1)), "replica") + EPSILON
    scaled = 2.0 * magnitude / ceiling - 1.0
    local_sums = chebyshev_sums(
        scaled.reshape(-1, shard_width), present.reshape(-1).astype(jnp.float32)
    )
    moments = lax.psum(local_sums, "replica")
    clip_level = ceiling * clip_fraction(moments, moments[0])
    calibrated = (jnp.clip(hidden, -clip_level, clip_level) / ceiling).astype(jnp.bfloat16)
    returned = lax.all_to_all(calibrated, "expert", split_axis=0, concat_axis=2, tiled=True)
    return returned.reshape(CAP, experts * HSPLIT * shard_width)


def solution(mesh):
    in_specs = (
        P(("expert", "replica"), None),
        P(("expert", "replica"), None),
        P(None, "expert"),
        P(None, "expert"),
    )
    out_specs = P(("expert", "replica"), None)
    return jax.shard_map(shards, mesh=mesh, in_specs=in_specs, out_specs=out_specs, check_vma=False)
```

profile of v0, /device:TPU:0, one launch (start us, length us, event | category | flops | bytes accessed | tf_op | source)
XLA Modules:
  0.0 88.1 jit_solution(15963084966948955778)
XLA Ops:
  0.0 0.7 convert_reduce_fusion
  0.7 0.6 reduce-window.6
  1.3 0.2 slice_reduce_fusion
  1.6 0.2 reduce-window.9
  1.8 0.2 select_reduce_fusion
  2.0 0.6 copy.18
  2.6 5.2 %all-to-all-start.1 = ((bf16[8,1,16]{2,1,0:T(2,128)(2,1)}), bf16[8,1,16]{2,1,0:T(2,128)(2,1)S(1)}, u32[]{:S(2)}, u32[]{:S(2)}) async-start(bf16[8,1,16]{2,1,0:T(2,128)(2,1)} %copy.18), calls=%async_computation.1 | async-start | bytes 8192 | tf_op jit(solution)/shard_map/all_to_all | solution.py:74
  7.9 3.8 %gather_fusion = bf16[32,7168]{1,0:T(8,128)(2,1)S(1)} fusion(bf16[256,7168]{1,0:T(8,128)(2,1)} %param.4, s32[1024]{0:T(1024)S(1)} %pad_clamp_fusion), kind=kCustom, calls=%fused_computation | custom fusion | bytes 917632 | tf_op jit(solution)/shard_map/jit(_take)/gather | solution.py:63
  11.8 0.6 all-to-all-done.1
  12.4 1.4 %broadcast_in_dim.20 = bf16[2,4,16,7168]{3,2,1,0:T(8,128)(2,1)} broadcast(bf16[2,16,7168]{2,1,0:T(8,128)(2,1)S(1)} %select_multiply_fusion), dimensions={0,2,3} | broadcast | bytes 2293760 | tf_op jit(solution)/shard_map/broadcast_in_dim | solution.py:65
  13.8 3.6 %all-to-all-start = ((bf16[8,16,7168]{2,1,0:T(8,128)(2,1)}), bf16[8,16,7168]{2,1,0:T(8,128)(2,1)S(1)}, u32[]{:S(2)}, u32[]{:S(2)}) async-start(bf16[8,16,7168]{2,1,0:T(8,128)(2,1)} %bitcast.45), calls=%async_computation | async-start | bytes 3670016 | tf_op jit(solution)/shard_map/all_to_all | solution.py:67
  17.5 0.6 convert_reduce_fusion.1
  18.2 23.0 %all-to-all-done = bf16[8,16,7168]{2,1,0:T(8,128)(2,1)S(1)} async-done(((bf16[8,16,7168]{2,1,0:T(8,128)(2,1)}), bf16[8,16,7168]{2,1,0:T(8,128)(2,1)S(1)}, u32[]{:S(2)}, u32[]{:S(2)}) %all-to-all-start) | async-done | bytes 1835040 | tf_op jit(solution)/shard_map/all_to_all | solution.py:67
  41.2 4.2 %fusion.8 = f32[128,512]{1,0:T(8,128)S(1)} fusion(bf16[128,7168]{1,0:T(8,128)(2,1)S(1)} %bitcast.43, bf16[7168,512]{1,0:T(8,128)(2,1)} %param.6), kind=kOutput, calls=%fused_computation.60 | convolution fusion | flops 939524096 | bytes 9437184 | tf_op jit(solution)/shard_map/dot_general | solution.py:69
  45.5 4.2 %abs_reduce_fusion = (f32[512]{0:T(512)S(1)}, f32[128,512]{1,0:T(8,128)S(1)}) fusion(bf16[128,7168]{1,0:T(8,128)(2,1)S(1)} %bitcast.44, bf16[7168,512]{1,0:T(8,128)(2,1)} %param.7, f32[128,512]{1,0:T(8,128)S(1)} %fusion.8), kind=kOutput, calls=%fused_computation.25 | convolution fusion | flops 939982336 | bytes 9701376 | tf_op jit(solution)/shard_map/dot_general | solution.py:70
  49.7 12.0 %pmax.7 = f32[512]{0:T(512)S(1)} all-reduce(f32[512]{0:T(512)S(1)} %get-tuple-element.22), channel_id=1, replica_groups=mesh['expert'=8,'replica'=4] {'replica'}, use_global_device_ids=true, to_apply=%region_6.7 | all-reduce | flops 512 | bytes 4096 | tf_op jit(solution)/shard_map/pmax | solution.py:77
  61.7 0.5 multiply_reduce_fusion
  62.1 0.6 stack.39
  62.9 15.8 %psum.7 = f32[12,512]{1,0:T(8,128)S(1)} all-reduce(f32[12,512]{1,0:T(8,128)S(1)} %stack.51), channel_id=1, replica_groups=mesh['expert'=8,'replica'=4] {'replica'}, use_global_device_ids=true, to_apply=%region_19.20 | all-reduce | flops 6144 | bytes 49152 | tf_op jit(solution)/shard_map/psum | solution.py:82
  78.8 0.2 fusion.2
  79.0 0.2 fusion.3
  79.2 0.2 fusion.4
  79.6 7.9 %all_to_all.29 = bf16[8,16,512]{2,1,0:T(8,128)(2,1)S(1)} all-to-all(bf16[8,16,512]{2,1,0:T(8,128)(2,1)S(1)} %divide_convert_fusion), channel_id=1, replica_groups=mesh['expert'=8,'replica'=4] {'expert'}, dimensions={0} | all-to-all | bytes 262144 | tf_op jit(solution)/shard_map/all_to_all | solution.py:85
  87.5 0.7 copy.21
  (22 shorter events, 0.7 us)
Async XLA Ops:
  2.6 9.8 %all-to-all-start.1 = ((bf16[8,1,16]{2,1,0:T(2,128)(2,1)}), bf16[8,1,16]{2,1,0:T(2,128)(2,1)S(1)}, u32[]{:S(2)}, u32[]{:S(2)}) async-start(bf16[8,1,16]{2,1,0:T(2,128)(2,1)} %copy.18), calls=%async_computation.1 | async-start | bytes 8192 | tf_op jit(solution)/shard_map/all_to_all | solution.py:74
  13.8 27.4 %all-to-all-start = ((bf16[8,16,7168]{2,1,0:T(8,128)(2,1)}), bf16[8,16,7168]{2,1,0:T(8,128)(2,1)S(1)}, u32[]{:S(2)}, u32[]{:S(2)}) async-start(bf16[8,16,7168]{2,1,0:T(8,128)(2,1)} %bitcast.45), calls=%async_computation | async-start | bytes 3670016 | tf_op jit(solution)/shard_map/all_to_all | solution.py:67
where the time goes:
time: 88.6 us; the launch traced here: 88.1 us
  blocking collectives  35.6 us (40%)
  waiting for transfers between devices  23.7 us (27%)
  starting transfers between devices  8.79 us (10%)
  matrix products  8.45 us (10%)
  local copies, waits for them, and re-layouts  7.57 us (9%)
  other arithmetic  3.88 us (4%)
    all_to_all x1, waiting for transfers between devices, shards(): lax.all_to_all(outgoing, 'expert', split_axis=0, concat_axis=0, tiled=True)  23 us
    psum x1, blocking collectives, shards(): moments = lax.psum(local_sums, 'replica')  15.8 us
    pmax x1, blocking collectives, shards(): ceiling = lax.pmax(jnp.max(magnitude, axis=(0, 1)), 'replica') + EPSILON  12 us
    all_to_all x1, blocking collectives, shards(): lax.all_to_all(calibrated, 'expert', split_axis=0, concat_axis=2, tiled=T...  7.89 us
    all_to_all x1, starting transfers between devices, shards(): lax.all_to_all(presence, 'expert', split_axis=0, concat_axis=0, tiled=True)  5.2 us
    dot_general x1, matrix products, shards(): up_act = jnp.dot(flat_rows, up_weight, preferred_element_type=jnp.float32)  4.23 us
    dot_general x1, matrix products, shards(): jnp.dot(flat_rows, gate_weight, preferred_element_type=jnp.float32)  4.22 us
    gather x1, local copies, waits for them, and re-layouts, shards(): jnp.take(tokens, picked.reshape(-1), axis=0).reshape(experts, CAP, D)  3.76 us
  transfers between devices with their start and end apart: 2, of which 2 were waited for; matrix products, arithmetic and copies ran while one was open for 5% of the time, Pallas kernels for 0%

commit v1 on v0

--- a/solution.py
+++ b/solution.py
@@ -79,7 +79,10 @@
     local_sums = chebyshev_sums(
         scaled.reshape(-1, shard_width), present.reshape(-1).astype(jnp.float32)
     )
-    moments = lax.psum(local_sums, "replica")
+    size, moments = (lax.axis_size("replica"), local_sums)
+    for hop in [1 << k for k in range(size.bit_length() - 1)]:
+        swap = [(i, i ^ hop) for i in range(size)]
+        moments = moments + lax.ppermute(moments, "replica", swap)
     clip_level = ceiling * clip_fraction(moments, moments[0])
     calibrated = (jnp.clip(hidden, -clip_level, clip_level) / ceiling).astype(jnp.bfloat16)
     returned = lax.all_to_all(calibrated, "expert", split_axis=0, concat_axis=2, tiled=True)

time: 88.6 us -> 81.6 us (0.921)
  blocking collectives: 35.6 us -> 19.9 us
  waiting for transfers between devices: 23.7 us -> 32.4 us
    psum x1 -> x0, blocking collectives: 15.8 us -> none  [shards(): moments = lax.psum(local_sums, 'replica')]
    ppermute x0 -> x2, waiting for transfers between devices: none -> 8.65 us  [shards(): moments = moments + lax.ppermute(moments, 'replica', swap)]
  transfers between devices with their start and end apart: 2 -> 4, of which waited for: 2 -> 4; matrix products, arithmetic and copies ran while one was open for 5% -> 6% of each run, Pallas kernels for 0% -> 0%
where the time goes in v1:
time: 81.6 us; the launch traced here: 81.1 us
  waiting for transfers between devices  32.4 us (40%)
  blocking collectives  19.9 us (24%)
  starting transfers between devices  8.86 us (11%)
  matrix products  8.45 us (10%)
  local copies, waits for them, and re-layouts  7.57 us (9%)
  other arithmetic  3.9 us (5%)
    all_to_all x1, waiting for transfers between devices, shards(): lax.all_to_all(outgoing, 'expert', split_axis=0, concat_axis=0, tiled=True)  23.1 us
    pmax x1, blocking collectives, shards(): ceiling = lax.pmax(jnp.max(magnitude, axis=(0, 1)), 'replica') + EPSILON  12 us
    ppermute x2, waiting for transfers between devices, shards(): moments = moments + lax.ppermute(moments, 'replica', swap)  8.65 us
    all_to_all x1, blocking collectives, shards(): lax.all_to_all(calibrated, 'expert', split_axis=0, concat_axis=2, tiled=T...  7.89 us
    all_to_all x1, starting transfers between devices, shards(): lax.all_to_all(presence, 'expert', split_axis=0, concat_axis=0, tiled=True)  5.2 us
    dot_general x1, matrix products, shards(): up_act = jnp.dot(flat_rows, up_weight, preferred_element_type=jnp.float32)  4.23 us
    dot_general x1, matrix products, shards(): jnp.dot(flat_rows, gate_weight, preferred_element_type=jnp.float32)  4.22 us
    gather x1, local copies, waits for them, and re-layouts, shards(): jnp.take(tokens, picked.reshape(-1), axis=0).reshape(experts, CAP, D)  3.76 us
  transfers between devices with their start and end apart: 4, of which 4 were waited for; matrix products, arithmetic and copies ran while one was open for 6% of the time, Pallas kernels for 0%

profile of v1, /device:TPU:0, one launch (start us, length us, event | category | flops | bytes accessed | tf_op | source)
XLA Modules:
  0.0 81.1 jit_solution(14671711066721324593)
XLA Ops:
  0.0 0.7 convert_reduce_fusion
  0.7 0.6 reduce-window.6
  1.3 0.2 slice_reduce_fusion
  1.6 0.2 reduce-window.9
  2.0 0.6 copy.18
  2.6 5.2 %all-to-all-start.1 = ((bf16[8,1,16]{2,1,0:T(2,128)(2,1)}), bf16[8,1,16]{2,1,0:T(2,128)(2,1)S(1)}, u32[]{:S(2)}, u32[]{:S(2)}) async-start(bf16[8,1,16]{2,1,0:T(2,128)(2,1)} %copy.18), calls=%async_computation.1 | async-start | bytes 8192 | tf_op jit(solution)/shard_map/all_to_all | solution.py:74
  7.9 3.8 %gather_fusion = bf16[32,7168]{1,0:T(8,128)(2,1)S(1)} fusion(bf16[256,7168]{1,0:T(8,128)(2,1)} %param.4, s32[1024]{0:T(1024)S(1)} %pad_clamp_fusion), kind=kCustom, calls=%fused_computation | custom fusion | bytes 917632 | tf_op jit(solution)/shard_map/jit(_take)/gather | solution.py:63
  11.8 0.6 all-to-all-done.1
  12.4 1.4 %broadcast_in_dim.20 = bf16[2,4,16,7168]{3,2,1,0:T(8,128)(2,1)} broadcast(bf16[2,16,7168]{2,1,0:T(8,128)(2,1)S(1)} %select_multiply_fusion), dimensions={0,2,3} | broadcast | bytes 2293760 | tf_op jit(solution)/shard_map/broadcast_in_dim | solution.py:65
  13.8 3.6 %all-to-all-start = ((bf16[8,16,7168]{2,1,0:T(8,128)(2,1)}), bf16[8,16,7168]{2,1,0:T(8,128)(2,1)S(1)}, u32[]{:S(2)}, u32[]{:S(2)}) async-start(bf16[8,16,7168]{2,1,0:T(8,128)(2,1)} %bitcast.45), calls=%async_computation | async-start | bytes 3670016 | tf_op jit(solution)/shard_map/all_to_all | solution.py:67
  17.4 0.6 convert_reduce_fusion.1
  18.1 23.1 %all-to-all-done = bf16[8,16,7168]{2,1,0:T(8,128)(2,1)S(1)} async-done(((bf16[8,16,7168]{2,1,0:T(8,128)(2,1)}), bf16[8,16,7168]{2,1,0:T(8,128)(2,1)S(1)}, u32[]{:S(2)}, u32[]{:S(2)}) %all-to-all-start) | async-done | bytes 1835040 | tf_op jit(solution)/shard_map/all_to_all | solution.py:67
  41.2 4.2 %fusion.8 = f32[128,512]{1,0:T(8,128)S(1)} fusion(bf16[128,7168]{1,0:T(8,128)(2,1)S(1)} %bitcast.43, bf16[7168,512]{1,0:T(8,128)(2,1)} %param.6), kind=kOutput, calls=%fused_computation.60 | convolution fusion | flops 939524096 | bytes 9437184 | tf_op jit(solution)/shard_map/dot_general | solution.py:69
  45.5 4.2 %abs_reduce_fusion = (f32[512]{0:T(512)S(1)}, f32[128,512]{1,0:T(8,128)S(1)}) fusion(bf16[128,7168]{1,0:T(8,128)(2,1)S(1)} %bitcast.44, bf16[7168,512]{1,0:T(8,128)(2,1)} %param.7, f32[128,512]{1,0:T(8,128)S(1)} %fusion.8), kind=kOutput, calls=%fused_computation.25 | convolution fusion | flops 939982336 | bytes 9701376 | tf_op jit(solution)/shard_map/dot_general | solution.py:70
  49.7 12.0 %pmax.7 = f32[512]{0:T(512)S(1)} all-reduce(f32[512]{0:T(512)S(1)} %get-tuple-element.22), channel_id=1, replica_groups=mesh['expert'=8,'replica'=4] {'replica'}, use_global_device_ids=true, to_apply=%region_6.7 | all-reduce | flops 512 | bytes 4096 | tf_op jit(solution)/shard_map/pmax | solution.py:77
  61.7 0.5 multiply_reduce_fusion
  62.1 0.6 stack.39
  63.0 3.9 %collective-permute-done = f32[12,512]{1,0:T(8,128)S(1)} collective-permute-done((f32[12,512]{1,0:T(8,128)S(1)}, f32[12,512]{1,0:T(8,128)S(1)}, u32[]{:S(2)}, u32[]{:S(2)}) %collective-permute-start) | collective-permute-done | bytes 24608 | tf_op jit(solution)/shard_map/ppermute | solution.py:85
  66.9 4.8 %collective-permute-done.1 = f32[12,512]{1,0:T(8,128)S(1)} collective-permute-done((f32[12,512]{1,0:T(8,128)S(1)}, f32[12,512]{1,0:T(8,128)S(1)}, u32[]{:S(2)}, u32[]{:S(2)}) %collective-permute-start.1) | collective-permute-done | bytes 24608 | tf_op jit(solution)/shard_map/ppermute | solution.py:85
  71.8 0.2 fusion.2
  72.0 0.2 fusion.3
  72.3 0.2 fusion.4
  72.6 7.9 %all_to_all.29 = bf16[8,16,512]{2,1,0:T(8,128)(2,1)S(1)} all-to-all(bf16[8,16,512]{2,1,0:T(8,128)(2,1)S(1)} %divide_convert_fusion), channel_id=1, replica_groups=mesh['expert'=8,'replica'=4] {'expert'}, dimensions={0} | all-to-all | bytes 262144 | tf_op jit(solution)/shard_map/all_to_all | solution.py:88
  80.5 0.7 copy.21
  (27 shorter events, 1.0 us)
Async XLA Ops:
  2.6 9.8 %all-to-all-start.1 = ((bf16[8,1,16]{2,1,0:T(2,128)(2,1)}), bf16[8,1,16]{2,1,0:T(2,128)(2,1)S(1)}, u32[]{:S(2)}, u32[]{:S(2)}) async-start(bf16[8,1,16]{2,1,0:T(2,128)(2,1)} %copy.18), calls=%async_computation.1 | async-start | bytes 8192 | tf_op jit(solution)/shard_map/all_to_all | solution.py:74
  13.8 27.4 %all-to-all-start = ((bf16[8,16,7168]{2,1,0:T(8,128)(2,1)}), bf16[8,16,7168]{2,1,0:T(8,128)(2,1)S(1)}, u32[]{:S(2)}, u32[]{:S(2)}) async-start(bf16[8,16,7168]{2,1,0:T(8,128)(2,1)} %bitcast.45), calls=%async_computation | async-start | bytes 3670016 | tf_op jit(solution)/shard_map/all_to_all | solution.py:67
  62.9 4.0 %collective-permute-start = (f32[12,512]{1,0:T(8,128)S(1)}, f32[12,512]{1,0:T(8,128)S(1)}, u32[]{:S(2)}, u32[]{:S(2)}) collective-permute-start(f32[12,512]{1,0:T(8,128)S(1)} %stack.51), channel_id=1, source_target_pairs={{0,1},{1,0},{2,3},{3,2},{4,5},{5,4},{6,7},{7,6},{8,9},{9,8},{10,11... | collective-permute-start | bytes 73736 | tf_op jit(solution)/shard_map/ppermute | solution.py:85
  66.9 4.8 %collective-permute-start.1 = (f32[12,512]{1,0:T(8,128)S(1)}, f32[12,512]{1,0:T(8,128)S(1)}, u32[]{:S(2)}, u32[]{:S(2)}) collective-permute-start(f32[12,512]{1,0:T(8,128)S(1)} %add.112), channel_id=1, source_target_pairs={{0,2},{1,3},{2,0},{3,1},{4,6},{5,7},{6,4},{7,5},{8,10},{9,11},{10,... | collective-permute-start | bytes 73736 | tf_op jit(solution)/shard_map/ppermute | solution.py:85
